TPU v7x, 256 devices: a whole 4x4x8 slice. The times are simulated.
256 devices in a mesh: dp: 4 (over x), row: 8 (over z_lo, core), col: 8 (over z_hi, y).
Axes of the slice: x: 4, y: 4, z: 8 (z_hi: 2, z_lo: 4; z = z_hi * 4 + z_lo), core: 2. Of those that a mesh axis runs over, the one named last changes fastest.
Arguments:
- tokens: bfloat16 [4096, 8192], P(('dp', 'col'), 'row'), may hold values from -6 to 6
- gate_weight: bfloat16 [8192, 14336], P('row', ('dp', 'col')), may hold values from -0.0625 to 0.0625
- up_weight: bfloat16 [8192, 14336], P('row', ('dp', 'col')), may hold values from -0.0625 to 0.0625
- down_weight: bfloat16 [14336, 8192], P(('dp', 'col'), 'row'), may hold values from -0.046875 to 0.046875
Outputs:
- mixed: bfloat16 [4096, 8192], P(('dp', 'col'), 'row')
All inputs are finite; a program needn't handle non-finite values.
Results may differ from a plain program's by a relative error of at most 0.03.
Values may be sent and summed in bfloat16 or wider, within the bound.
A program may use at most 64 MiB of HBM per device.

v0:
```python
import jax
import jax.numpy as jnp
from jax import lax
from jax.sharding import PartitionSpec as P


def on_device(tokens, gate_weight, up_weight, down_weight):
    group_tokens = lax.all_gather(tokens, "col", axis=0, tiled=True)
    gate_cols, up_cols = (
        lax.all_gather(gate_weight, "dp", axis=1, tiled=True),
        lax.all_gather(up_weight, "dp", axis=1, tiled=True),
    )
    gate_term = jnp.dot(group_tokens, gate_cols, preferred_element_type=jnp.float32)
    up_term = jnp.dot(group_tokens, up_cols, preferred_element_type=jnp.float32)
    row_sums = lax.psum_scatter(
        jnp.concatenate((gate_term, up_term), axis=1).astype(jnp.bfloat16),
        "row",
        scatter_dimension=0,
        tiled=True,
    ).astype(jnp.float32)
    half_width = gate_cols.shape[1]
    gate_sum = row_sums[:, :half_width]
    up_sum = row_sums[:, half_width:]
    hidden = (jax.nn.silu(gate_sum) * up_sum).astype(jnp.bfloat16)
    hidden_all = lax.all_gather(hidden, "row", axis=0, tiled=True)
    down_term = jnp.dot(
        hidden_all,
        lax.all_gather(down_weight, "dp", axis=0, tiled=True),
        preferred_element_type=jnp.float32,
    )
    mixed = lax.psum_scatter(down_term.astype(jnp.bfloat16), "col", scatter_dimension=0, tiled=True)
    return mixed


def solution(mesh):
    return jax.shard_map(
        on_device,
        mesh=mesh,
        in_specs=(
            P(("dp", "col"), "row"),
            P("row", ("dp", "col")),
            P("row", ("dp", "col")),
            P(("dp", "col"), "row"),
        ),
        out_specs=P(("dp", "col"), "row"),
        check_vma=False,
    )
```

profile of v0, /device:TPU:2, one launch (start us, length us, event | category | flops | bytes accessed | tf_op | source)
XLA Modules:
  0.0 489.1 jit_solution(3508342044773073556)
XLA Ops:
  6.5 0.0 all-gather.6.cloned.1.call-start
  6.5 0.7 all-gather.6.cloned.1.call-update
  7.3 0.0 all-gather.8.cloned.1.call-start
  7.3 0.7 all-gather.8.cloned.1.call-update
  8.0 0.0 all-gather.10.cloned.1.call-start
  8.1 0.7 all-gather.10.cloned.1.call-update
  8.7 0.0 reduce-scatter.3.cloned.1.call-start
  8.8 80.1 %all-gather.6.cloned.1.call-done = bf16[1024,1024]{1,0:T(8,128)(2,1)} async-done(((bf16[128,1024]{1,0:T(8,128)(2,1)}), bf16[1024,1024]{1,0:T(8,128)(2,1)}) %all-gather.6.cloned.1.call-update) | async-done | bytes 2097168 | tf_op jit(solution)/shard_map/all_gather | solution.py:8
  88.9 43.2 %all-gather.8.cloned.1.call-done = bf16[1024,1792]{0,1:T(8,128)(2,1)} async-done(((bf16[1024,448]{0,1:T(8,128)(2,1)}), bf16[1024,1792]{0,1:T(8,128)(2,1)}) %all-gather.8.cloned.1.call-update) | async-done | bytes 3670032 | tf_op jit(solution)/shard_map/all_gather | solution.py:10
  132.1 8.5 %convolution_convert_fusion.1 = bf16[1024,1792]{1,0:T(8,128)(2,1)} fusion(bf16[1024,1024]{1,0:T(8,128)(2,1)} %all-gather.6.cloned.1.call-done, bf16[1024,1792]{0,1:T(8,128)(2,1)} %all-gather.8.cloned.1.call-done), kind=kOutput, calls=%fused_computation.2 | convolution fusion | flops 3759931392 | bytes 9437184 | tf_op jit(solution)/shard_map/dot_general | solution.py:13
  140.6 40.0 %all-gather.10.cloned.1.call-done = bf16[1024,1792]{0,1:T(8,128)(2,1)} async-done(((bf16[1024,448]{0,1:T(8,128)(2,1)}), bf16[1024,1792]{0,1:T(8,128)(2,1)}) %all-gather.10.cloned.1.call-update) | async-done | bytes 3670032 | tf_op jit(solution)/shard_map/all_gather | solution.py:11
  180.6 0.0 copy-start
  180.6 8.7 %convolution_convert_fusion = bf16[1024,1792]{1,0:T(8,128)(2,1)} fusion(bf16[1024,1024]{1,0:T(8,128)(2,1)} %all-gather.6.cloned.1.call-done, bf16[1024,1792]{0,1:T(8,128)(2,1)} %all-gather.10.cloned.1.call-done), kind=kOutput, calls=%fused_computation.1 | convolution fusion | flops 3759931392 | bytes 9437184 | tf_op jit(solution)/shard_map/dot_general | solution.py:14
  189.3 0.0 copy-done
  189.3 5.5 %pad_maximum_fusion = bf16[1024,3584]{1,0:T(8,128)(2,1)} fusion(bf16[1024,1792]{1,0:T(8,128)(2,1)} %convolution_convert_fusion, bf16[1024,1792]{1,0:T(8,128)(2,1)S(1)} %copy-done), kind=kLoop, calls=%fused_computation | loop fusion | flops 14680064 | bytes 14680064 | tf_op jit(solution)/shard_map/concatenate | solution.py:16
  194.8 0.0 reduce-scatter.3.cloned.1.call-update
  194.9 0.0 all-gather.14.cloned.1.call-start
  194.9 0.5 all-gather.14.cloned.1.call-update
  195.5 0.0 all-gather.12.cloned.1.call-start
  195.5 85.4 %reduce-scatter.3.cloned.1.call-done = bf16[128,3584]{1,0:T(8,128)(2,1)} async-done(((bf16[1024,3584]{1,0:T(8,128)(2,1)}), bf16[128,3584]{1,0:T(8,128)(2,1)}) %reduce-scatter.3.cloned.1.call-update) | async-done | bytes 917520 | tf_op jit(solution)/shard_map/reduce_scatter | solution.py:15
  280.9 1.4 convert_element_type.10
  282.3 1.0 fusion
  283.3 0.0 all-gather.12.cloned.1.call-update
  283.3 0.0 reduce-scatter.5.cloned.1.call-start
  283.4 43.5 %all-gather.14.cloned.1.call-done = bf16[1792,1024]{1,0:T(8,128)(2,1)} async-done(((bf16[448,1024]{1,0:T(8,128)(2,1)}), bf16[1792,1024]{1,0:T(8,128)(2,1)}) %all-gather.14.cloned.1.call-update) | async-done | bytes 3670032 | tf_op jit(solution)/shard_map/all_gather | solution.py:28
  326.9 52.3 %all-gather.12.cloned.1.call-done = bf16[1024,1792]{1,0:T(8,128)(2,1)} async-done(((bf16[128,1792]{1,0:T(8,128)(2,1)}), bf16[1024,1792]{1,0:T(8,128)(2,1)}) %all-gather.12.cloned.1.call-update) | async-done | bytes 3670032 | tf_op jit(solution)/shard_map/all_gather | solution.py:25
  379.2 8.4 %convolution_convert_fusion.2 = bf16[1024,1024]{1,0:T(8,128)(2,1)} fusion(bf16[1024,1792]{1,0:T(8,128)(2,1)} %all-gather.12.cloned.1.call-done, bf16[1792,1024]{1,0:T(8,128)(2,1)} %all-gather.14.cloned.1.call-done), kind=kOutput, calls=%fused_computation.3 | convolution fusion | flops 3759144960 | bytes 9437184 | tf_op jit(solution)/shard_map/dot_general | solution.py:26
  387.6 0.0 reduce-scatter.5.cloned.1.call-update
  387.6 94.6 %reduce-scatter.5.cloned.1.call-done = bf16[128,1024]{1,0:T(8,128)(2,1)} async-done(((bf16[1024,1024]{1,0:T(8,128)(2,1)}), bf16[128,1024]{1,0:T(8,128)(2,1)}) %reduce-scatter.5.cloned.1.call-update) | async-done | bytes 262160 | tf_op jit(solution)/shard_map/reduce_scatter | solution.py:31
Async XLA Ops:
  6.5 82.4 %all-gather.6.cloned.1.call-start = ((), (), s32[]{:S(2)}) async-start(), calls=%async_computation.2 | async-start | bytes 2359296 | tf_op jit(solution)/shard_map/all_gather | solution.py:8
  7.3 124.9 %all-gather.8.cloned.1.call-start = ((), (), s32[]{:S(2)}) async-start(), calls=%async_computation.3 | async-start | bytes 4587520 | tf_op jit(solution)/shard_map/all_gather | solution.py:10
  8.0 172.6 %all-gather.10.cloned.1.call-start = ((), (), s32[]{:S(2)}) async-start(), calls=%async_computation.4 | async-start | bytes 4587520 | tf_op jit(solution)/shard_map/all_gather | solution.py:11
  8.7 272.2 %reduce-scatter.3.cloned.1.call-start = ((), (), s32[]{:S(2)}) async-start(), calls=%async_computation.5 | async-start | bytes 8257536 | tf_op jit(solution)/shard_map/reduce_scatter | solution.py:15
  180.6 8.7 %copy-start = (bf16[1024,1792]{1,0:T(8,128)(2,1)S(1)}, bf16[1024,1792]{1,0:T(8,128)(2,1)}, u32[]{:S(2)}) copy-start(bf16[1024,1792]{1,0:T(8,128)(2,1)} %convolution_convert_fusion.1) | copy-start | bytes 11010052
  194.9 132.0 %all-gather.14.cloned.1.call-start = ((), (), s32[]{:S(2)}) async-start(), calls=%async_computation.7 | async-start | bytes 4587520 | tf_op jit(solution)/shard_map/all_gather | solution.py:28
  195.5 183.7 %all-gather.12.cloned.1.call-start = ((), (), s32[]{:S(2)}) async-start(), calls=%async_computation.6 | async-start | bytes 4128768 | tf_op jit(solution)/shard_map/all_gather | solution.py:25
  283.3 198.9 %reduce-scatter.5.cloned.1.call-start = ((), (), s32[]{:S(2)}) async-start(), calls=%async_computation.8 | async-start | bytes 2359296 | tf_op jit(solution)/shard_map/reduce_scatter | solution.py:31
Sparse Core Ops, SparseCore 0:
  10.0 78.8 all-gather.5
  90.7 41.3 all-gather.7
  133.9 46.6 all-gather.9
  195.0 85.8 reduce-scatter.2
  282.6 44.2 all-gather.13
  328.5 50.5 all-gather.11
  387.7 94.4 reduce-scatter.4
where the time goes:
time: 489 us
  waiting for transfers between devices  442 us (90%)
  matrix products  25.7 us (5%)
  between operations  13.5 us (3%)
  other arithmetic  7.89 us (2%)
    reduce_scatter x1, waiting for transfers between devices, on_device(): lax.psum_scatter(down_term.astype(jnp.bfloat16), 'col', scatter_dimension...  94.6 us
    reduce_scatter x1, waiting for transfers between devices, on_device(): lax.psum_scatter(jnp.concatenate((gate_term, up_term), axis=1).astype(jnp...  85.4 us
    all_gather x1, waiting for transfers between devices, on_device(): group_tokens = lax.all_gather(tokens, 'col', axis=0, tiled=True)  80.1 us
    all_gather x1, waiting for transfers between devices, on_device(): hidden_all = lax.all_gather(hidden, 'row', axis=0, tiled=True)  52.3 us
    all_gather x1, waiting for transfers between devices, on_device(): lax.all_gather(down_weight, 'dp', axis=0, tiled=True)  43.5 us
    all_gather x1, waiting for transfers between devices, on_device(): lax.all_gather(gate_weight, 'dp', axis=1, tiled=True)  43.2 us
    all_gather x1, waiting for transfers between devices, on_device(): lax.all_gather(up_weight, 'dp', axis=1, tiled=True)  40 us
  transfers between devices with their start and end apart: 7, of which 7 were waited for; matrix products, arithmetic and copies ran while one was open for 2% of the time, Pallas kernels for 0%

commit v1 on v0

--- a/solution.py
+++ b/solution.py
@@ -4,10 +4,26 @@
 from jax.sharding import PartitionSpec as P
 
 
+def gather_around(x, axis, dim):
+    ways, here, turn = (lax.axis_size(axis), lax.axis_index(axis), x.shape[dim])
+    shape = [n * ways if d == dim else n for d, n in enumerate(x.shape)]
+    full = lax.dynamic_update_slice_in_dim(jnp.zeros(shape, x.dtype), x, here * turn, axis=dim)
+    going_up = going_down = x
+    for far in range(1, ways // 2 + 1):
+        going_up = lax.ppermute(going_up, axis, [(d, (d + 1) % ways) for d in range(ways)])
+        full = lax.dynamic_update_slice_in_dim(full, going_up, (here - far) % ways * turn, axis=dim)
+        if 2 * far < ways:
+            going_down = lax.ppermute(going_down, axis, [(d, (d - 1) % ways) for d in range(ways)])
+            full = lax.dynamic_update_slice_in_dim(
+                full, going_down, (here + far) % ways * turn, axis=dim
+            )
+    return full
+
+
 def on_device(tokens, gate_weight, up_weight, down_weight):
     group_tokens = lax.all_gather(tokens, "col", axis=0, tiled=True)
     gate_cols, up_cols = (
-        lax.all_gather(gate_weight, "dp", axis=1, tiled=True),
+        gather_around(gate_weight, "dp", 1),
         lax.all_gather(up_weight, "dp", axis=1, tiled=True),
     )
     gate_term = jnp.dot(group_tokens, gate_cols, preferred_element_type=jnp.float32)

time: 489 us -> 452 us (0.924)
  waiting for transfers between devices: 442 us -> 382 us
  local copies, waits for them, and re-layouts: 0.01 us -> 19.1 us
    reduce_scatter x1 -> x0, waiting for transfers between devices: 85.4 us -> none  [on_device(): lax.psum_scatter(jnp.concatenate((gate_term, up_term), axis=1).astype(jnp...]
    unnamed x7, waiting for transfers between devices: 2.67 us -> 87.2 us
    all_gather x1, waiting for transfers between devices: 80.1 us -> 36.4 us  [on_device(): group_tokens = lax.all_gather(tokens, 'col', axis=0, tiled=True)]
    all_gather x1 -> x0, waiting for transfers between devices: 43.2 us -> none  [on_device(): lax.all_gather(gate_weight, 'dp', axis=1, tiled=True)]
    ppermute x0 -> x3, waiting for transfers between devices: none -> 33 us  [the longest x2 33 us: gather_around(): lax.ppermute(going_up, axis, [(d, (d + 1) % ways) for d in range(ways)])]
    unnamed x2 -> x6, local copies, waits for them, and re-layouts: 0.01 us -> 11.5 us
    all_gather x1, waiting for transfers between devices: 40 us -> 34.6 us  [on_device(): lax.all_gather(up_weight, 'dp', axis=1, tiled=True)]
    dynamic_update_slice x0 -> x4, local copies, waits for them, and re-layouts: none -> 5.22 us  [the longest x1 2.18 us: gather_around(): lax.dynamic_update_slice_in_dim(full, going_down, (here + far) % ways * t...]
  transfers between devices with their start and end apart: 7 -> 9, of which waited for: 7 -> 8; matrix products, arithmetic and copies ran while one was open for 2% -> 4% of each run, Pallas kernels for 0% -> 0%
where the time goes in v1:
time: 452 us; the launch traced here: 451 us
  waiting for transfers between devices  382 us (85%)
  matrix products  25.8 us (6%)
  local copies, waits for them, and re-layouts  19.1 us (4%)
  between operations  13.5 us (3%)
  other arithmetic  7.03 us (2%)
    reduce_scatter x1, waiting for transfers between devices, on_device(): lax.psum_scatter(down_term.astype(jnp.bfloat16), 'col', scatter_dimension...  96.4 us
    unnamed x7, waiting for transfers between devices  87.2 us
    all_gather x1, waiting for transfers between devices, on_device(): hidden_all = lax.all_gather(hidden, 'row', axis=0, tiled=True)  50.8 us
    all_gather x1, waiting for transfers between devices, on_device(): lax.all_gather(down_weight, 'dp', axis=0, tiled=True)  43.2 us
    all_gather x1, waiting for transfers between devices, on_device(): group_tokens = lax.all_gather(tokens, 'col', axis=0, tiled=True)  36.4 us
    all_gather x1, waiting for transfers between devices, on_device(): lax.all_gather(up_weight, 'dp', axis=1, tiled=True)  34.6 us
    ppermute x2, waiting for transfers between devices, gather_around(): lax.ppermute(going_up, axis, [(d, (d + 1) % ways) for d in range(ways)])  33 us
    unnamed x6, local copies, waits for them, and re-layouts  11.5 us
  transfers between devices with their start and end apart: 9, of which 8 were waited for; matrix products, arithmetic and copies ran while one was open for 4% of the time, Pallas kernels for 0%

profile of v1, /device:TPU:2, one launch (start us, length us, event | category | flops | bytes accessed | tf_op | source)
XLA Modules:
  0.0 451.3 jit_solution(12194176516375075834)
XLA Ops:
  6.5 0.7 all-gather.5.cloned.1.call-update
  7.3 0.0 all-gather.7.cloned.1.call-start
  7.3 0.7 all-gather.7.cloned.1.call-update
  8.0 0.0 reduce-scatter.7.cloned.1.call-start
  8.1 1.6 collective-permute-start
  9.6 0.8 collective-permute-start.1
  10.5 20.0 %collective-permute-done = bf16[1024,448]{0,1:T(8,128)(2,1)S(1)} collective-permute-done((bf16[1024,448]{0,1:T(8,128)(2,1)}, bf16[1024,448]{0,1:T(8,128)(2,1)S(1)}, u32[]{:S(2)}, u32[]{:S(2)}) %collective-permute-start) | collective-permute-done | bytes 917536 | tf_op jit(solution)/shard_map/ppermute | solution.py:13
  30.4 1.5 collective-permute-start.2
  31.9 2.3 broadcast_in_dim.3
  34.2 1.0 constant_dynamic-update-slice_fusion.3
  35.3 1.0 constant_dynamic-update-slice_fusion.2
  36.3 2.2 constant_dynamic-update-slice_fusion.1
  38.5 13.1 %collective-permute-done.2 = bf16[1024,448]{0,1:T(8,128)(2,1)S(1)} collective-permute-done((bf16[1024,448]{0,1:T(8,128)(2,1)S(1)}, bf16[1024,448]{0,1:T(8,128)(2,1)S(1)}, u32[]{:S(2)}, u32[]{:S(2)}) %collective-permute-start.2) | collective-permute-done | bytes 917536 | tf_op jit(solution)/shard_map/ppermute | solution.py:13
  51.5 1.0 constant_dynamic-update-slice_fusion
  52.5 36.4 %all-gather.5.cloned.1.call-done = bf16[1024,1024]{1,0:T(8,128)(2,1)} async-done(((bf16[128,1024]{1,0:T(8,128)(2,1)}), bf16[1024,1024]{1,0:T(8,128)(2,1)}) %all-gather.5.cloned.1.call-update) | async-done | bytes 2097168 | tf_op jit(solution)/shard_map/all_gather | solution.py:24
  88.9 8.6 %fusion = bf16[1024,1792]{0,1:T(8,128)(2,1)} fusion(bf16[1024,1792]{0,1:T(8,128)(2,1)} %constant_dynamic-update-slice_fusion, bf16[1024,1024]{1,0:T(8,128)(2,1)} %all-gather.5.cloned.1.call-done), kind=kOutput, calls=%fused_computation.3 | convolution fusion | flops 3759931392 | bytes 9437184 | tf_op jit(solution)/shard_map/dot_general | solution.py:29
  97.5 34.6 %all-gather.7.cloned.1.call-done = bf16[1024,1792]{0,1:T(8,128)(2,1)} async-done(((bf16[1024,448]{0,1:T(8,128)(2,1)}), bf16[1024,1792]{0,1:T(8,128)(2,1)}) %all-gather.7.cloned.1.call-update) | async-done | bytes 3670032 | tf_op jit(solution)/shard_map/all_gather | solution.py:27
  132.1 8.7 %convolution_convert_fusion = bf16[1024,1792]{0,1:T(8,128)(2,1)} fusion(bf16[1024,1024]{1,0:T(8,128)(2,1)} %all-gather.5.cloned.1.call-done, bf16[1024,1792]{0,1:T(8,128)(2,1)} %all-gather.7.cloned.1.call-done), kind=kOutput, calls=%fused_computation.1 | convolution fusion | flops 3759931392 | bytes 9437184 | tf_op jit(solution)/shard_map/dot_general | solution.py:30
  140.8 5.9 %pad_maximum_fusion = bf16[1024,3584]{0,1:T(8,128)(2,1)} fusion(bf16[1024,1792]{0,1:T(8,128)(2,1)} %convolution_convert_fusion, bf16[1024,1792]{0,1:T(8,128)(2,1)S(1)} %copy-done), kind=kLoop, calls=%fused_computation | loop fusion | flops 14680064 | bytes 14680064 | tf_op jit(solution)/shard_map/concatenate | solution.py:32
  146.7 10.0 %copy.8 = bf16[1024,3584]{1,0:T(8,128)(2,1)} copy(bf16[1024,3584]{0,1:T(8,128)(2,1)} %pad_maximum_fusion) | data formatting | bytes 14680064
  156.7 0.0 all-gather.11.cloned.1.call-start
  156.8 0.5 all-gather.11.cloned.1.call-update
  157.3 0.2 all-gather.9.cloned.1.call-start
  157.5 85.2 %reduce-scatter.7.cloned.1.call-done = bf16[128,3584]{1,0:T(8,128)(2,1)} async-done(((bf16[1024,3584]{1,0:T(8,128)(2,1)}), bf16[128,3584]{1,0:T(8,128)(2,1)}) %reduce-scatter.7.cloned.1.call-update) | async-done | bytes 917520
  242.8 1.5 copy.9
  244.3 0.1 convert_element_type.10
  244.5 1.0 fusion.1
  245.5 0.0 reduce-scatter.5.cloned.1.call-start
  245.5 43.2 %all-gather.11.cloned.1.call-done = bf16[1792,1024]{1,0:T(8,128)(2,1)} async-done(((bf16[448,1024]{1,0:T(8,128)(2,1)}), bf16[1792,1024]{1,0:T(8,128)(2,1)}) %all-gather.11.cloned.1.call-update) | async-done | bytes 3670032 | tf_op jit(solution)/shard_map/all_gather | solution.py:44
  288.7 50.8 %all-gather.9.cloned.1.call-done = bf16[1024,1792]{0,1:T(8,128)(2,1)} async-done(((bf16[128,1792]{0,1:T(8,128)(2,1)}), bf16[1024,1792]{0,1:T(8,128)(2,1)}) %all-gather.9.cloned.1.call-update) | async-done | bytes 3670032 | tf_op jit(solution)/shard_map/all_gather | solution.py:41
  339.5 8.5 %convolution_convert_fusion.2 = bf16[1024,1024]{1,0:T(8,128)(2,1)} fusion(bf16[1024,1792]{0,1:T(8,128)(2,1)} %all-gather.9.cloned.1.call-done, bf16[1792,1024]{1,0:T(8,128)(2,1)} %all-gather.11.cloned.1.call-done), kind=kOutput, calls=%fused_computation.4 | convolution fusion | flops 3759144960 | bytes 9437184 | tf_op jit(solution)/shard_map/dot_general | solution.py:42
  348.1 96.4 %reduce-scatter.5.cloned.1.call-done = bf16[128,1024]{1,0:T(8,128)(2,1)} async-done(((bf16[1024,1024]{1,0:T(8,128)(2,1)}), bf16[128,1024]{1,0:T(8,128)(2,1)}) %reduce-scatter.5.cloned.1.call-update) | async-done | bytes 262160 | tf_op jit(solution)/shard_map/reduce_scatter | solution.py:47
  (9 shorter events, 0.1 us)
Async XLA Ops:
  6.5 27.7 %copy-start.1 = (bf16[1024,448]{0,1:T(8,128)(2,1)S(1)}, bf16[1024,448]{0,1:T(8,128)(2,1)}, u32[]{:S(2)}) copy-start(bf16[1024,448]{0,1:T(8,128)(2,1)} %param.5) | copy-start | bytes 2752516
  6.5 82.4 %all-gather.5.cloned.1.call-start = ((), (), s32[]{:S(2)}) async-start(), calls=%async_computation.2 | async-start | bytes 2359296 | tf_op jit(solution)/shard_map/all_gather | solution.py:24
  7.3 124.9 %all-gather.7.cloned.1.call-start = ((), (), s32[]{:S(2)}) async-start(), calls=%async_computation.3 | async-start | bytes 4587520 | tf_op jit(solution)/shard_map/all_gather | solution.py:27
  8.0 234.8 %reduce-scatter.7.cloned.1.call-start = ((), (), s32[]{:S(2)}) async-start(), calls=%async_computation.7 | async-start | bytes 8257536
  8.1 22.4 %collective-permute-start = (bf16[1024,448]{0,1:T(8,128)(2,1)}, bf16[1024,448]{0,1:T(8,128)(2,1)S(1)}, u32[]{:S(2)}, u32[]{:S(2)}) collective-permute-start(bf16[1024,448]{0,1:T(8,128)(2,1)} %param.5), channel_id=1, source_target_pairs={{0,64},{64,128},{128,192},{192,0},{1,65},{65,129},{129,193},{193,1... | collective-permute-start | bytes 2752520 | tf_op jit(solution)/shard_map/ppermute | solution.py:13
  9.6 26.7 %collective-permute-start.1 = (bf16[1024,448]{0,1:T(8,128)(2,1)}, bf16[1024,448]{0,1:T(8,128)(2,1)}, u32[]{:S(2)}, u32[]{:S(2)}) collective-permute-start(bf16[1024,448]{0,1:T(8,128)(2,1)} %param.5), channel_id=1, source_target_pairs={{0,192},{64,0},{128,64},{192,128},{1,193},{65,1},{129,65},{193,129... | collective-permute-start | bytes 2752520 | tf_op jit(solution)/shard_map/ppermute | solution.py:16
  30.4 21.1 %collective-permute-start.2 = (bf16[1024,448]{0,1:T(8,128)(2,1)S(1)}, bf16[1024,448]{0,1:T(8,128)(2,1)S(1)}, u32[]{:S(2)}, u32[]{:S(2)}) collective-permute-start(bf16[1024,448]{0,1:T(8,128)(2,1)S(1)} %collective-permute-done), channel_id=1, source_target_pairs={{0,64},{64,128},{128,192},{192,0},{1,65},{65,129},{129,193},{193,1... | collective-permute-start | bytes 2752520 | tf_op jit(solution)/shard_map/ppermute | solution.py:13
  132.1 8.7 %copy-start = (bf16[1024,1792]{0,1:T(8,128)(2,1)S(1)}, bf16[1024,1792]{0,1:T(8,128)(2,1)}, u32[]{:S(2)}) copy-start(bf16[1024,1792]{0,1:T(8,128)(2,1)} %fusion) | copy-start | bytes 11010052
  156.7 132.0 %all-gather.11.cloned.1.call-start = ((), (), s32[]{:S(2)}) async-start(), calls=%async_computation.5 | async-start | bytes 4587520 | tf_op jit(solution)/shard_map/all_gather | solution.py:44
  157.3 182.2 %all-gather.9.cloned.1.call-start = ((), (), s32[]{:S(2)}) async-start(), calls=%async_computation.4 | async-start | bytes 4128768 | tf_op jit(solution)/shard_map/all_gather | solution.py:41
  245.5 199.0 %reduce-scatter.5.cloned.1.call-start = ((), (), s32[]{:S(2)}) async-start(), calls=%async_computation.6 | async-start | bytes 2359296 | tf_op jit(solution)/shard_map/reduce_scatter | solution.py:47
Sparse Core Ops, SparseCore 0:
  10.0 78.8 all-gather.4
  90.7 41.3 all-gather.6
  156.8 85.8 reduce-scatter.6
  244.4 44.2 all-gather.10
  290.3 49.1 all-gather.8
  348.2 96.2 reduce-scatter.4
